TPU v7x, 128 devices: a whole 4x4x4 slice. The times are simulated.
128 devices in a mesh: depth: 8 (over x, core), width: 16 (over y, z).
Axes of the slice: x: 4, y: 4, z: 4, core: 2. Of those that a mesh axis runs over, the one named last changes fastest.
Arguments:
- thermal_field: float32 [128, 256, 2048], P('depth', None, 'width'), may hold values from 1 to 3
- particulate_fraction: bfloat16 [128, 256, 2048], P('depth', None, 'width'), may hold values from 0 to 1
- sootiness_extinction: float32 [8], replicated, may hold values from 0.02 to 0.3
- vapour_extinction_rate: float32 [8], replicated, may hold values from 0.02 to 0.2
- planck_over_wavelength: float32 [8], replicated, may hold values from 2 to 8
- layer_sightline_position: int32 [8], replicated, may hold values from 0 to 7, each once
- picture_adjoint_seed: float32 [8, 256, 2048], P(None, ('depth', 'width')), may hold values from -6 to 6
Outputs:
- radiance: float32 [8, 256, 2048], P(None, ('depth', 'width'))
- temperature_gradient: float32 [128, 256, 2048], P('depth', None, 'width')
Inputs may be any that keep to these rules, and one draw needn't show every extreme that they name: `layer_sightline_position`: each slab position occurs exactly once.
All inputs are finite; a program needn't handle non-finite values.
Results may differ from a plain program's by a relative error of at most 0.0003.
Values sent between devices are 32-bit elements; how exact they have to be, the bound alone decides.
A program may use at most 192 MiB of HBM per device.

v0:
```python
import math

import jax
import jax.numpy as jnp
from jax import lax
from jax.experimental import pallas as pl
from jax.experimental.pallas import tpu as pltpu
from jax.sharding import PartitionSpec as P

NB = 8
CD = 16
SLABS = 8
ROWS = 32
LANES = 128
LOG2E = math.log2(math.e)
VMEM = pltpu.CompilerParams(vmem_limit_bytes=48 << 20)


def light_kernel(co, t_ref, p_ref, out_ref, pf):
    for k in range(CD):
        pf[k] = p_ref[k].astype(jnp.float32)

    @pl.loop(0, ROWS // 8)
    def _(i):
        rows = pl.ds(pl.multiple_of(i * 8, 8), 8)
        pp = jnp.zeros((8, LANES), jnp.float32)
        tt = jnp.zeros((8, LANES), jnp.float32)
        before = [jnp.ones((8, LANES), jnp.float32)] * NB
        light = [jnp.zeros((8, LANES), jnp.float32)] * NB
        for k in range(CD):
            t = t_ref[k, rows, :]
            pp = pp + pf[k, rows, :]
            tt = tt + t
            inv = 1.0 / t
            for b in range(NB):
                r = 1.0 / (jnp.exp2(co[2, b] * inv) - 1.0)
                behind = jnp.exp2(co[0, b] * pp + co[1, b] * tt)
                light[b] = light[b] + (before[b] - behind) * r
                before[b] = behind
        for b in range(NB):
            out_ref[b, rows, :] = light[b] * co[5, b]
        out_ref[NB, rows, :] = pp
        out_ref[NB + 1, rows, :] = tt


def grad_kernel(co, t_ref, p_ref, w_ref, g_ref, pf):
    for k in range(CD):
        pf[k] = p_ref[k].astype(jnp.float32)

    @pl.loop(0, ROWS // 8)
    def _(i):
        rows = pl.ds(pl.multiple_of(i * 8, 8), 8)
        pp = jnp.zeros((8, LANES), jnp.float32)
        tt = jnp.zeros((8, LANES), jnp.float32)
        before = [jnp.ones((8, LANES), jnp.float32)] * NB
        y = [jnp.zeros((8, LANES), jnp.float32)] * NB
        last = [jnp.zeros((8, LANES), jnp.float32)] * NB
        seen = [w_ref[b, rows, :] for b in range(NB)]
        w1 = [seen[b] * co[3, b] for b in range(NB)]
        w2 = [seen[b] * co[4, b] for b in range(NB)]
        q = w_ref[NB, rows, :]
        for k in range(CD):
            t = t_ref[k, rows, :]
            pp = pp + pf[k, rows, :]
            tt = tt + t
            inv = 1.0 / t
            s = -q
            v = jnp.zeros((8, LANES), jnp.float32)
            for b in range(NB):
                r = 1.0 / (jnp.exp2(co[2, b] * inv) - 1.0)
                behind = jnp.exp2(co[0, b] * pp + co[1, b] * tt)
                y[b] = y[b] + before[b] * (r - last[b])
                x = (before[b] - behind) * (r * (r + 1.0))
                s = s + w1[b] * y[b]
                v = v + w2[b] * x
                before[b] = behind
                last[b] = r
            g_ref[k, rows, :] = s + v * (inv * inv)


def compose_kernel(pos, co, got_ref, seed_ref, rad_ref, back_ref):
    front = [
        [jnp.where(pos[i] < pos[j], 1.0, 0.0) for j in range(SLABS)] for i in range(SLABS)
    ]

    @pl.loop(0, ROWS // 8)
    def _(i):
        rows = pl.ds(pl.multiple_of(i * 8, 8), 8)
        ps = [got_ref[NB, s, rows, :] for s in range(SLABS)]
        ts = [got_ref[NB + 1, s, rows, :] for s in range(SLABS)]
        pp = [sum(front[a][s] * ps[a] for a in range(SLABS) if a != s) for s in range(SLABS)]
        tt = [sum(front[a][s] * ts[a] for a in range(SLABS) if a != s) for s in range(SLABS)]
        q = [jnp.zeros((8, LANES), jnp.float32)] * SLABS
        for b in range(NB):
            seed = seed_ref[b, rows, :]
            weight = seed * co[6, b]
            faded = []
            for s in range(SLABS):
                dim = jnp.exp2(co[0, b] * pp[s] + co[1, b] * tt[s])
                back_ref[b, s, rows, :] = seed * dim
                faded.append(dim * got_ref[b, s, rows, :])
            rad_ref[b, rows, :] = sum(faded)
            for s in range(SLABS):
                rest = faded[s]
                for a in range(SLABS):
                    if a != s:
                        rest = rest + front[s][a] * faded[a]
                q[s] = q[s] + weight * rest
        for s in range(SLABS):
            back_ref[NB, s, rows, :] = q[s]


def on_device(
    thermal_field,
    particulate_fraction,
    sootiness_extinction,
    vapour_extinction_rate,
    planck_over_wavelength,
    layer_sightline_position,
    picture_adjoint_seed,
):
    gas = vapour_extinction_rate / CD
    scale = jnp.exp(0.5 * planck_over_wavelength) - 1.0
    co = jnp.stack(
        [
            sootiness_extinction * (-LOG2E / CD),
            vapour_extinction_rate * (-LOG2E / CD),
            planck_over_wavelength * LOG2E,
            scale * gas,
            scale * planck_over_wavelength,
            scale,
            gas,
        ]
    )
    f32 = jnp.float32
    lines = thermal_field.shape[1]
    smem = pl.BlockSpec(memory_space=pltpu.SMEM)
    cells = pl.BlockSpec((CD, ROWS, LANES), lambda i: (0, i, 0))
    sent = pl.pallas_call(
        light_kernel,
        grid=(lines // ROWS,),
        out_shape=jax.ShapeDtypeStruct((NB + 2, lines, LANES), f32),
        in_specs=[smem, cells, cells],
        out_specs=pl.BlockSpec((NB + 2, ROWS, LANES), lambda i: (0, i, 0)),
        scratch_shapes=[pltpu.VMEM((CD, ROWS, LANES), f32)],
        compiler_params=VMEM,
    )(co, thermal_field, particulate_fraction)
    seeds = lax.all_to_all(
        picture_adjoint_seed.reshape(NB, 2, 16, LANES), "width", split_axis=2, concat_axis=1, tiled=True
    ).reshape(NB, ROWS, LANES)
    got = lax.all_to_all(
        sent.reshape(NB + 2, SLABS, ROWS, LANES), "depth", split_axis=1, concat_axis=1, tiled=True
    )
    radiance, back = pl.pallas_call(
        compose_kernel,
        out_shape=(
            jax.ShapeDtypeStruct((NB, ROWS, LANES), f32),
            jax.ShapeDtypeStruct((NB + 1, SLABS, ROWS, LANES), f32),
        ),
        in_specs=[smem, smem] + [pl.BlockSpec(memory_space=pltpu.VMEM)] * 2,
        out_specs=(pl.BlockSpec(memory_space=pltpu.VMEM),) * 2,
        compiler_params=VMEM,
    )(layer_sightline_position, co, got, seeds)
    weights = lax.all_to_all(back, "depth", split_axis=1, concat_axis=1, tiled=True).reshape(
        NB + 1, lines, LANES
    )
    radiance = lax.all_to_all(
        radiance.reshape(NB, ROWS, 1, LANES), "width", split_axis=1, concat_axis=2, tiled=True
    ).reshape(NB, 2, 16 * LANES)
    gradient = pl.pallas_call(
        grad_kernel,
        grid=(lines // ROWS,),
        out_shape=jax.ShapeDtypeStruct((CD, lines, LANES), f32),
        in_specs=[smem, cells, cells, pl.BlockSpec((NB + 1, ROWS, LANES), lambda i: (0, i, 0))],
        out_specs=cells,
        scratch_shapes=[pltpu.VMEM((CD, ROWS, LANES), f32)],
        compiler_params=VMEM,
    )(co, thermal_field, particulate_fraction, weights)
    return radiance, gradient


def solution(mesh):
    placed = (
        P("depth", None, "width"),
        P("depth", None, "width"),
        P(),
        P(),
        P(),
        P(),
        P(None, ("depth", "width"), None),
    )
    return jax.shard_map(
        on_device,
        mesh=mesh,
        in_specs=placed,
        out_specs=(P(None, ("depth", "width"), None), P("depth", None, "width")),
        check_vma=False,
    )
```

profile of v0, /device:TPU:1, one launch (start us, length us, event | category | flops | bytes accessed | tf_op | source)
XLA Modules:
  0.0 102.6 jit_solution(217372386349754703)
XLA Ops:
  0.6 0.0 copy-start
  0.6 0.9 copy-done
  1.5 0.7 copy_bitcast_fusion
  2.2 8.6 %all-to-all-start.1 = ((f32[8,2,16,128]{3,1,0,2:T(2,128)}), f32[8,2,16,128]{3,1,0,2:T(2,128)S(1)}, u32[]{:S(2)}, u32[]{:S(2)}) async-start(f32[8,2,16,128]{3,1,0,2:T(2,128)} %copy_bitcast_fusion), calls=%async_computation.1 | async-start | bytes 262144 | tf_op jit(solution)/shard_map/all_to_all | solution.py:148
  10.8 0.7 multiply_bitcast_fusion.5
  11.5 0.7 multiply_bitcast_fusion.4
  12.2 1.6 %copy-done.1 = f32[16,256,128]{2,1,0:T(8,128)S(1)} copy-done((f32[16,256,128]{2,1,0:T(8,128)S(1)}, f32[16,256,128]{2,1,0:T(8,128)}, u32[]{:S(2)}) %copy-start.1) | copy-done | bytes 2097176
  13.8 1.2 %copy-done.3 = bf16[16,256,128]{2,1,0:T(8,128)(2,1)S(1)} copy-done((bf16[16,256,128]{2,1,0:T(8,128)(2,1)S(1)}, bf16[16,256,128]{2,1,0:T(8,128)(2,1)}, u32[]{:S(2)}) %copy-start.3) | copy-done | bytes 1048600
  15.0 8.5 %shard_map.86 = f32[10,256,128]{2,1,0:T(8,128)S(1)} custom-call(f32[7,8]{1,0:T(8,128)S(1)} %stack.31.co, f32[16,256,128]{2,1,0:T(8,128)S(1)} %copy-done.1, bf16[16,256,128]{2,1,0:T(8,128)(2,1)S(1)} %copy-done.3), custom_call_target="tpu_custom_call" | custom-call | tf_op jit(solution)/shard_map/pallas_call | solution.py:139
  23.5 1.2 %copy.18 = f32[10,8,32,128]{3,2,0,1:T(8,128)} copy(f32[10,8,32,128]{3,2,1,0:T(8,128)S(1)} %bitcast.33) | data formatting | bytes 2621440 | tf_op jit(solution)/shard_map/reshape | solution.py:152
  24.7 5.3 %all-to-all-start = ((f32[10,8,32,128]{3,2,0,1:T(8,128)}), f32[10,8,32,128]{3,2,0,1:T(8,128)S(1)}, u32[]{:S(2)}, u32[]{:S(2)}) async-start(f32[10,8,32,128]{3,2,0,1:T(8,128)} %copy.18), calls=%async_computation | async-start | bytes 2621440 | tf_op jit(solution)/shard_map/all_to_all | solution.py:151
  30.0 17.7 %all-to-all-done = f32[10,8,32,128]{3,2,0,1:T(8,128)S(1)} async-done(((f32[10,8,32,128]{3,2,0,1:T(8,128)}), f32[10,8,32,128]{3,2,0,1:T(8,128)S(1)}, u32[]{:S(2)}, u32[]{:S(2)}) %all-to-all-start) | async-done | bytes 1310752 | tf_op jit(solution)/shard_map/all_to_all | solution.py:151
  47.8 0.1 copy.22.got_ref
  47.9 1.7 %shard_map.87 = (f32[8,32,128]{2,1,0:T(8,128)S(1)}, f32[9,8,32,128]{3,2,1,0:T(8,128)S(1)}) custom-call(s32[8]{0:T(128)S(1)} %copy-done.5, f32[7,8]{1,0:T(8,128)S(1)} %stack.31.co, f32[10,8,32,128]{3,2,1,0:T(8,128)S(1)} %copy.22.got_ref, f32[8,32,128]{2,1,0:T(8,128)S(1)} %bitcast.35), custom_call_target="tpu_custom_call" | custom-call | tf_op jit(solution)/shard_map/pallas_call | solution.py:154
  49.6 0.7 copy.23
  50.3 6.9 %all-to-all-start.2 = ((f32[8,32,1,128]{3,0,2,1:T(8,128)}), f32[8,32,1,128]{3,0,2,1:T(8,128)S(1)}, u32[]{:S(2)}, u32[]{:S(2)}) async-start(f32[8,32,1,128]{3,0,2,1:T(8,128)} %copy.23), calls=%async_computation.2 | async-start | bytes 262144 | tf_op jit(solution)/shard_map/all_to_all | solution.py:167
  57.2 1.1 %copy.25 = f32[9,8,32,128]{3,2,0,1:T(8,128)} copy(f32[9,8,32,128]{3,2,1,0:T(8,128)S(1)} %get-tuple-element.5) | data formatting | bytes 2359296 | tf_op jit(solution)/shard_map/pallas_call | solution.py:154
  58.3 5.6 %all-to-all-done.2 = f32[8,32,1,128]{3,0,2,1:T(8,128)S(1)} async-done(((f32[8,32,1,128]{3,0,2,1:T(8,128)}), f32[8,32,1,128]{3,0,2,1:T(8,128)S(1)}, u32[]{:S(2)}, u32[]{:S(2)}) %all-to-all-start.2) | async-done | bytes 131104 | tf_op jit(solution)/shard_map/all_to_all | solution.py:167
  63.9 6.7 %all-to-all-start.3 = ((f32[9,8,32,128]{3,2,0,1:T(8,128)}), f32[9,8,32,128]{3,2,0,1:T(8,128)}, u32[]{:S(2)}, u32[]{:S(2)}) async-start(f32[9,8,32,128]{3,2,0,1:T(8,128)} %copy.25), calls=%async_computation.3 | async-start | bytes 2359296 | tf_op jit(solution)/shard_map/all_to_all | solution.py:164
  70.7 0.0 copy-start.2
  70.7 0.7 reshape.28
  71.4 15.7 %all-to-all-done.3 = f32[9,8,32,128]{3,2,0,1:T(8,128)} async-done(((f32[9,8,32,128]{3,2,0,1:T(8,128)}), f32[9,8,32,128]{3,2,0,1:T(8,128)}, u32[]{:S(2)}, u32[]{:S(2)}) %all-to-all-start.3) | async-done | bytes 1179680 | tf_op jit(solution)/shard_map/all_to_all | solution.py:164
  87.1 1.4 %copy.26 = f32[9,8,32,128]{3,2,1,0:T(8,128)S(1)} copy(f32[9,8,32,128]{3,2,0,1:T(8,128)} %all-to-all-done.3) | data formatting | bytes 2359296 | tf_op jit(solution)/shard_map/all_to_all | solution.py:164
  88.5 14.1 %shard_map.88 = f32[16,256,128]{2,1,0:T(8,128)} custom-call(f32[7,8]{1,0:T(8,128)S(1)} %stack.31.co, f32[16,256,128]{2,1,0:T(8,128)S(1)} %copy-done.2, bf16[16,256,128]{2,1,0:T(8,128)(2,1)S(1)} %copy-done.4, f32[9,256,128]{2,1,0:T(8,128)S(1)} %bitcast.34), custom_call_target="tpu_custom_call" | custom-call | tf_op jit(solution)/shard_map/pallas_call | solution.py:170
  (11 shorter events, 0.1 us)
Async XLA Ops:
  0.6 0.9 copy-start
  2.2 22.5 %all-to-all-start.1 = ((f32[8,2,16,128]{3,1,0,2:T(2,128)}), f32[8,2,16,128]{3,1,0,2:T(2,128)S(1)}, u32[]{:S(2)}, u32[]{:S(2)}) async-start(f32[8,2,16,128]{3,1,0,2:T(2,128)} %copy_bitcast_fusion), calls=%async_computation.1 | async-start | bytes 262144 | tf_op jit(solution)/shard_map/all_to_all | solution.py:148
  12.2 1.6 %copy-start.1 = (f32[16,256,128]{2,1,0:T(8,128)S(1)}, f32[16,256,128]{2,1,0:T(8,128)}, u32[]{:S(2)}) copy-start(f32[16,256,128]{2,1,0:T(8,128)} %t_ref.3) | copy-start | bytes 6291460
  13.8 1.2 %copy-start.3 = (bf16[16,256,128]{2,1,0:T(8,128)(2,1)S(1)}, bf16[16,256,128]{2,1,0:T(8,128)(2,1)}, u32[]{:S(2)}) copy-start(bf16[16,256,128]{2,1,0:T(8,128)(2,1)} %p_ref.3) | copy-start | bytes 3145732
  24.7 23.0 %all-to-all-start = ((f32[10,8,32,128]{3,2,0,1:T(8,128)}), f32[10,8,32,128]{3,2,0,1:T(8,128)S(1)}, u32[]{:S(2)}, u32[]{:S(2)}) async-start(f32[10,8,32,128]{3,2,0,1:T(8,128)} %copy.18), calls=%async_computation | async-start | bytes 2621440 | tf_op jit(solution)/shard_map/all_to_all | solution.py:151
  30.0 17.9 %copy-start.5 = (s32[8]{0:T(128)S(1)}, s32[8]{0:T(128)}, u32[]{:S(2)}) copy-start(s32[8]{0:T(128)} %pos.1) | copy-start | bytes 100
  50.3 13.6 %all-to-all-start.2 = ((f32[8,32,1,128]{3,0,2,1:T(8,128)}), f32[8,32,1,128]{3,0,2,1:T(8,128)S(1)}, u32[]{:S(2)}, u32[]{:S(2)}) async-start(f32[8,32,1,128]{3,0,2,1:T(8,128)} %copy.23), calls=%async_computation.2 | async-start | bytes 262144 | tf_op jit(solution)/shard_map/all_to_all | solution.py:167
  63.9 24.6 %copy-start.4 = (bf16[16,256,128]{2,1,0:T(8,128)(2,1)S(1)}, bf16[16,256,128]{2,1,0:T(8,128)(2,1)}, u32[]{:S(2)}) copy-start(bf16[16,256,128]{2,1,0:T(8,128)(2,1)} %p_ref.3) | copy-start | bytes 3145732
  63.9 23.2 %all-to-all-start.3 = ((f32[9,8,32,128]{3,2,0,1:T(8,128)}), f32[9,8,32,128]{3,2,0,1:T(8,128)}, u32[]{:S(2)}, u32[]{:S(2)}) async-start(f32[9,8,32,128]{3,2,0,1:T(8,128)} %copy.25), calls=%async_computation.3 | async-start | bytes 2359296 | tf_op jit(solution)/shard_map/all_to_all | solution.py:164
  70.7 17.9 %copy-start.2 = (f32[16,256,128]{2,1,0:T(8,128)S(1)}, f32[16,256,128]{2,1,0:T(8,128)}, u32[]{:S(2)}) copy-start(f32[16,256,128]{2,1,0:T(8,128)} %t_ref.3) | copy-start | bytes 6291460
where the time goes:
time: 103 us
  waiting for transfers between devices  39 us (38%)
  starting transfers between devices  27.4 us (27%)
  Pallas kernels  24.3 us (24%)
  local copies, waits for them, and re-layouts  9.78 us (9%)
  other arithmetic  1.34 us (1%)
    all_to_all x1, waiting for transfers between devices, on_device(): lax.all_to_all(sent.reshape(NB + 2, SLABS, ROWS, LANES), 'depth', split_a...  17.7 us
    all_to_all x1, waiting for transfers between devices, on_device(): lax.all_to_all(back, 'depth', split_axis=1, concat_axis=1, tiled=True)  15.7 us
    pallas_call x1, Pallas kernels, on_device(): pl.pallas_call(grad_kernel, grid=(lines // ROWS,), out_shape=jax.ShapeDty...  14.1 us
    all_to_all x1, starting transfers between devices, on_device(): lax.all_to_all(picture_adjoint_seed.reshape(NB, 2, 16, LANES), 'width', s...  8.59 us
    pallas_call x1, Pallas kernels, on_device(): pl.pallas_call(light_kernel, grid=(lines // ROWS,), out_shape=jax.ShapeDt...  8.51 us
    all_to_all x1, starting transfers between devices, on_device(): lax.all_to_all(radiance.reshape(NB, ROWS, 1, LANES), 'width', split_axis=...  6.93 us
    all_to_all x1, starting transfers between devices, on_device(): lax.all_to_all(back, 'depth', split_axis=1, concat_axis=1, tiled=True)  6.67 us
    all_to_all x1, waiting for transfers between devices, on_device(): lax.all_to_all(radiance.reshape(NB, ROWS, 1, LANES), 'width', split_axis=...  5.59 us
  transfers between devices with their start and end apart: 4, of which 3 were waited for; matrix products, arithmetic and copies ran while one was open for 4% of the time, Pallas kernels for 8%

commit v1 on v0

v1 whole, which is shorter than its diff:
```python
import math

import jax
import jax.numpy as jnp
from jax import lax
from jax.experimental import pallas as pl
from jax.experimental.pallas import tpu as pltpu
from jax.sharding import PartitionSpec as P

MESH = pl.DeviceIdType.MESH
NB = 8
CD = 16
SLABS = 8
COLS = 16
CHIPS = 4
LINES = 256
ROWS = 32
LANES = 128
TILE = (8, LANES)
LOG2E = math.log2(math.e)
F32 = jnp.float32


def kernel(
    soot,
    vapour,
    planck,
    pos,
    t_hbm,
    p_hbm,
    seed_hbm,
    rad_out,
    grad_hbm,
    q_out,
    t_v,
    p_v,
    pf,
    big,
    table,
    sum_s,
    sum_r,
    fro_s,
    fro_r,
    seed_l,
    seed_a,
    lit,
    pair_r,
    chip_s,
    chip_r,
    gs_s,
    gs_r,
    q_s,
    q_r,
    rad_v,
    rad_s,
    rad_r,
    grad_v,
    in_sem,
    out_sem,
    sum_ss,
    sum_rs,
    fro_ss,
    fro_rs,
    seed_ss,
    seed_rs,
    sax_ss,
    sax_rs,
    sap_ss,
    sap_rs,
    pair_ss,
    pair_rs,
    chip_ss,
    chip_rs,
    gs_ss,
    gs_rs,
    q_ss,
    q_rs,
    rad_ss,
    rad_rs,
):
    d = lax.axis_index("depth")
    w = lax.axis_index("width")
    c = lax.rem(d, 2)
    x = d // 2
    pair = d + 1 - 2 * c

    def chip(i):
        return lax.rem(x + 1 + i, CHIPS)

    def tile_of(n):
        g = n // 4
        e = 2 * chip(g // 2) + lax.rem(g + 1 + c, 2)
        return e, pl.multiple_of(8 * lax.rem(n, 4), 8)

    def rdma(src, dst, ss, rs, dev):
        return pltpu.make_async_remote_copy(
            src_ref=src, dst_ref=dst, send_sem=ss, recv_sem=rs, device_id=dev, device_id_type=MESH
        )

    def loads(i):
        rows = pl.ds(pl.multiple_of(64 * chip(i), 64), 64)
        return (
            pltpu.make_async_copy(t_hbm.at[:, rows, :], t_v.at[:, rows, :], in_sem.at[0, i]),
            pltpu.make_async_copy(p_hbm.at[:, rows, :], p_v.at[:, rows, :], in_sem.at[1, i]),
        )

    for i in range(CHIPS):
        for cp in loads(i):
            cp.start()

    barrier = pltpu.get_barrier_semaphore()
    for o in range(1, SLABS):
        pl.semaphore_signal(
            barrier, inc=1, device_id={"depth": lax.rem(d + o, SLABS)}, device_id_type=MESH
        )
    for o in range(1, COLS):
        pl.semaphore_signal(
            barrier, inc=1, device_id={"width": lax.rem(w + o, COLS)}, device_id_type=MESH
        )

    ks = [soot[b] * (-LOG2E / CD) for b in range(NB)]
    kv = [vapour[b] * (-LOG2E / CD) for b in range(NB)]
    kp = [planck[b] * LOG2E for b in range(NB)]
    gas = [vapour[b] * (1.0 / CD) for b in range(NB)]
    front = [
        [jnp.where(pos[i] < pos[j], 1.0, 0.0) for j in range(SLABS)] for i in range(SLABS)
    ]
    for b in range(NB):
        scale = jnp.exp(jnp.full(TILE, 0.5 * planck[b], F32)) - 1.0
        table[0, b] = scale
        table[1, b] = scale * gas[b]
        table[2, b] = jnp.full(TILE, planck[b], F32) / gas[b]

    pl.semaphore_wait(barrier, SLABS + COLS - 2)

    def cols(i):
        return pl.ds(pl.multiple_of(i * LANES, LANES), LANES)

    def seed_copy(to, slot):
        return rdma(
            seed_hbm.at[:, cols(to)], seed_l.at[slot], seed_ss.at[to], seed_rs.at[slot], {"width": to}
        )

    @pl.loop(1, COLS)
    def _(o):
        seed_copy(lax.rem(w + o, COLS), w).start()

    seed_own = pltpu.make_async_copy(seed_hbm.at[:, cols(w)], seed_l.at[w], out_sem.at[SLABS])
    seed_own.start()

    def exchange(send, recv, ss, rs):
        def make(to, slot):
            return rdma(send.at[to], recv.at[slot], ss.at[to], rs.at[slot], {"depth": to})

        return make

    sums = exchange(sum_s, sum_r, sum_ss, sum_rs)
    fronts = exchange(fro_s, fro_r, fro_ss, fro_rs)
    grads = exchange(gs_s, gs_r, gs_ss, gs_rs)
    quots = exchange(q_s, q_r, q_ss, q_rs)

    def others():
        return [lax.rem(d + o, SLABS) for o in (2, 3, 4, 5, 6, 7, 1)]

    for i in range(CHIPS):
        for cp in loads(i):
            cp.wait()
        for half in range(2):
            e = 2 * chip(i) + lax.rem(half + 1 + c, 2)

            @pl.loop(0, 2)
            def _(j):
                r16 = pl.multiple_of(16 * j, 16)
                rows = pl.ds(pl.multiple_of(ROWS * e + r16, 16), 16)
                pp = jnp.zeros((16, LANES), F32)
                tt = jnp.zeros((16, LANES), F32)
                for k in range(CD):
                    p = p_v[k, rows, :].astype(F32)
                    pf[k, rows, :] = p
                    pp = pp + p
                    tt = tt + t_v[k, rows, :]
                if i == CHIPS - 1 and half == 1:
                    sum_r[d, 0, pl.ds(r16, 16), :] = pp
                    sum_r[d, 1, pl.ds(r16, 16), :] = tt
                else:
                    sum_s[e, 0, pl.ds(r16, 16), :] = pp
                    sum_s[e, 1, pl.ds(r16, 16), :] = tt

            if not (i == CHIPS - 1 and half == 1):
                sums(e, d).start()

    def heavy(n0, n1):
        @pl.loop(n0, n1)
        def _(n):
            e, r8 = tile_of(n)
            rows = pl.ds(pl.multiple_of(ROWS * e + r8, 8), 8)
            pp = jnp.zeros(TILE, F32)
            tt = jnp.zeros(TILE, F32)
            before = [None] * NB
            y = [None] * NB
            last = [None] * NB
            for k in range(CD):
                t = t_v[k, rows, :]
                pp = pp + pf[k, rows, :]
                tt = tt + t
                inv = 1.0 / t
                inv2 = inv * inv
                for b in range(NB):
                    r = 1.0 / (jnp.exp2(kp[b] * inv) - 1.0)
                    behind = jnp.exp2(ks[b] * pp + kv[b] * tt)
                    if k == 0:
                        y[b] = r
                        lost = 1.0 - behind
                    else:
                        y[b] = y[b] + before[b] * (r - last[b])
                        lost = before[b] - behind
                    big[b, k, rows, :] = y[b] + (lost * (r * (r + 1.0))) * (table[2, b] * inv2)
                    before[b] = behind
                    last[b] = r
            for b in range(NB):
                lit[e, pl.ds(ROWS * b + r8, 8), :] = (y[b] - before[b] * last[b]) * table[0, b]

    def make_fronts():
        for p in others():
            sums(p, p).wait_recv()

        @pl.loop(0, ROWS // 8)
        def _(j):
            rows = pl.ds(pl.multiple_of(8 * j, 8), 8)
            for h in range(2):
                part = [sum_r[s, h, rows, :] for s in range(SLABS)]
                for s in range(SLABS):
                    fro_s[s, h, rows, :] = sum(
                        front[a][s] * part[a] for a in range(SLABS) if a != s
                    )

        fro_r[d] = fro_s[d]
        for p in others():
            fronts(p, d).start()

    def same(i):
        return lax.rem(d + 2 * i, SLABS)

    def sax(to, slot):
        return rdma(
            seed_a.at[slot], seed_a.at[slot], sax_ss.at[to // 2], sax_rs.at[slot // 2], {"depth": to}
        )

    def sap(slot):
        return rdma(
            seed_a.at[slot], seed_a.at[slot], sap_ss.at[slot // 2], sap_rs.at[slot // 2], {"depth": pair}
        )

    def spread_seeds():
        @pl.loop(1, COLS)
        def _(o):
            p = lax.rem(w + o, COLS)
            seed_copy(p, p).wait_recv()

        seed_own.wait()
        for b in range(NB):
            for r in range(2):
                for h in range(2):
                    seed_a[d, pl.ds(ROWS * b + r + 16 * h, 8, stride=2), :] = seed_l[
                        pl.ds(8 * h, 8), 2 * b + r, :
                    ]
        for i in (2, 1, 3):
            sax(same(i), d).start()
        sap(d).start()

    def forward_seeds():
        for i in (1, 3, 2):
            sax(same(i), same(i)).wait_recv()
            sap(same(i)).start()

    def dims(e, r8):
        pp = fro_r[e, 0, pl.ds(r8, 8), :]
        tt = fro_r[e, 1, pl.ds(r8, 8), :]
        return [jnp.exp2(ks[b] * pp + kv[b] * tt) for b in range(NB)]

    def fade(n0, n1):
        @pl.loop(n0, n1)
        def _(n):
            e, r8 = tile_of(n)
            dim = dims(e, r8)
            for b in range(NB):
                rows = pl.ds(ROWS * b + r8, 8)
                lit[e, rows, :] = lit[e, rows, :] * dim[b]

    def pairs(i, slot):
        return rdma(
            lit.at[2 * chip(i) + 1 - c],
            pair_r.at[slot],
            pair_ss.at[i],
            pair_rs.at[slot],
            {"depth": pair},
        )

    def chips(i, slot):
        return rdma(
            chip_s.at[i], chip_r.at[slot], chip_ss.at[i], chip_rs.at[slot], {"depth": same(i + 1)}
        )

    def join(i):
        pairs(i, chip(i)).wait_recv()
        e = 2 * chip(i) + c

        @pl.loop(0, NB * ROWS // 8)
        def _(j):
            rows = pl.ds(pl.multiple_of(8 * j, 8), 8)
            chip_s[i, rows, :] = lit[e, rows, :] + pair_r[chip(i), rows, :]

    heavy(0, 12)
    make_fronts()
    heavy(12, 16)
    spread_seeds()
    heavy(16, 24)
    forward_seeds()
    for p in others():
        fronts(p, p).wait_recv()
    for i in range(3):
        fade(8 * i, 8 * i + 8)
        pairs(i, chip(i)).start()
    heavy(24, 28)
    for i in range(3):
        join(i)
        chips(i, x).start()
    heavy(28, 32)
    fade(24, 32)
    pairs(3, chip(3)).start()

    for s in range(CHIPS):
        sap(2 * s + 1 - c).wait_recv()

    @pl.loop(0, 32)
    def _(n):
        e, r8 = tile_of(n)
        total = jnp.zeros(TILE, F32)
        for b in range(NB):
            rows = pl.ds(ROWS * b + r8, 8)
            total = total + gas[b] * (seed_a[e, rows, :] * lit[e, rows, :])
        gs_s[e, pl.ds(r8, 8), :] = total

    gs_r[d] = gs_s[d]
    for p in others():
        grads(p, d).start()

    def out_copy(g):
        e, _ = tile_of(4 * g)
        rows = pl.ds(pl.multiple_of(ROWS * e, ROWS), ROWS)
        return pltpu.make_async_copy(
            grad_v.at[:, rows, :], grad_hbm.at[:, rows, :], out_sem.at[g]
        )

    def finish(g0, g1):
        @pl.loop(g0, g1)
        def _(g):
            @pl.loop(0, 4)
            def _(j):
                e, r8 = tile_of(4 * g + j)
                rows = pl.ds(pl.multiple_of(ROWS * e + r8, 8), 8)
                dim = dims(e, r8)
                wt = [
                    table[1, b] * (seed_a[e, pl.ds(ROWS * b + r8, 8), :] * dim[b])
                    for b in range(NB)
                ]
                for k in range(CD):
                    acc = wt[0] * big[0, k, rows, :]
                    for b in range(1, NB):
                        acc = acc + wt[b] * big[b, k, rows, :]
                    grad_v[k, rows, :] = acc

            out_copy(g).start()

    finish(0, 4)

    pairs(3, x).wait_recv()
    for i in range(3):
        chips(i, chip(i)).wait_recv()

    @pl.loop(0, NB * ROWS // 8)
    def _(j):
        rows = pl.ds(pl.multiple_of(8 * j, 8), 8)
        rad_v[rows, :] = (
            (lit[d, rows, :] + pair_r[x, rows, :])
            + (chip_r[chip(0), rows, :] + chip_r[chip(1), rows, :])
            + chip_r[chip(2), rows, :]
        )

    for b in range(NB):
        for r in range(2):
            for h in range(2):
                rad_s[pl.ds(8 * h, 8), 2 * b + r, :] = rad_v[
                    pl.ds(ROWS * b + r + 16 * h, 8, stride=2), :
                ]
    rad_r[:, cols(w)] = rad_s[w]

    def rad_copy(to, slot):
        return rdma(
            rad_s.at[to], rad_r.at[:, cols(slot)], rad_ss.at[to], rad_rs.at[slot], {"width": to}
        )

    @pl.loop(1, COLS)
    def _(o):
        rad_copy(lax.rem(w + o, COLS), w).start()

    for p in others():
        grads(p, p).wait_recv()

    @pl.loop(0, ROWS // 8)
    def _(j):
        rows = pl.ds(pl.multiple_of(8 * j, 8), 8)
        part = [gs_r[s, rows, :] for s in range(SLABS)]
        for s in range(SLABS):
            rest = part[s]
            for a in range(SLABS):
                if a != s:
                    rest = rest + front[s][a] * part[a]
            q_s[s, rows, :] = rest

    q_r[d] = q_s[d]
    for p in others():
        quots(p, d).start()
    finish(4, 8)

    for p in others():
        quots(p, p).wait_recv()
    q_out[...] = q_r[...]

    @pl.loop(1, COLS)
    def _(o):
        p = lax.rem(w + o, COLS)
        rad_copy(p, p).wait_recv()

    rad_out[...] = rad_r[...]
    for g in range(SLABS):
        out_copy(g).wait()
    for p in others():
        sums(p, d).wait_send()
        fronts(p, d).wait_send()
        grads(p, d).wait_send()
        quots(p, d).wait_send()
    for i in (1, 2, 3):
        sax(same(i), d).wait_send()
    for s in range(CHIPS):
        sap(2 * s + c).wait_send()
        pairs(s, chip(s)).wait_send()
    for i in range(3):
        chips(i, x).wait_send()

    @pl.loop(1, COLS)
    def _(o):
        p = lax.rem(w + o, COLS)
        seed_copy(p, w).wait_send()
        rad_copy(p, w).wait_send()


def on_device(
    thermal_field,
    particulate_fraction,
    sootiness_extinction,
    vapour_extinction_rate,
    planck_over_wavelength,
    layer_sightline_position,
    picture_adjoint_seed,
):
    smem = pl.BlockSpec(memory_space=pltpu.SMEM)
    vmem = pl.BlockSpec(memory_space=pltpu.VMEM)
    hbm = pl.BlockSpec(memory_space=pl.ANY)

    def v(*shape):
        return pltpu.VMEM(shape, F32)

    def sems(*shape):
        return pltpu.SemaphoreType.DMA(shape)

    field = (CD, LINES, LANES)
    image = (NB * ROWS, LANES)
    radiance, gradient, quot = pl.pallas_call(
        kernel,
        out_shape=(
            jax.ShapeDtypeStruct((2 * NB, COLS * LANES), F32),
            jax.ShapeDtypeStruct(field, F32),
            jax.ShapeDtypeStruct((SLABS, ROWS, LANES), F32),
        ),
        in_specs=[smem, smem, smem, smem, hbm, hbm, hbm],
        out_specs=(vmem, hbm, vmem),
        scratch_shapes=[
            v(*field),
            pltpu.VMEM(field, jnp.bfloat16),
            v(*field),
            v(NB, *field),
            v(3, NB, *TILE),
            v(SLABS, 2, ROWS, LANES),
            v(SLABS, 2, ROWS, LANES),
            v(SLABS, 2, ROWS, LANES),
            v(SLABS, 2, ROWS, LANES),
            v(COLS, 2 * NB, LANES),
            v(SLABS, *image),
            v(SLABS, *image),
            v(CHIPS, *image),
            v(3, *image),
            v(CHIPS, *image),
            v(SLABS, ROWS, LANES),
            v(SLABS, ROWS, LANES),
            v(SLABS, ROWS, LANES),
            v(SLABS, ROWS, LANES),
            v(*image),
            v(COLS, 2 * NB, LANES),
            v(2 * NB, COLS * LANES),
            v(*field),
            sems(2, CHIPS),
            sems(SLABS + 1),
            sems(SLABS),
            sems(SLABS),
            sems(SLABS),
            sems(SLABS),
            sems(COLS),
            sems(COLS),
            sems(CHIPS),
            sems(CHIPS),
            sems(CHIPS),
            sems(CHIPS),
            sems(CHIPS),
            sems(CHIPS),
            sems(3),
            sems(CHIPS),
            sems(SLABS),
            sems(SLABS),
            sems(SLABS),
            sems(SLABS),
            sems(COLS),
            sems(COLS),
        ],
        compiler_params=pltpu.CompilerParams(
            collective_id=0, has_side_effects=True, vmem_limit_bytes=56 << 20
        ),
    )(
        sootiness_extinction,
        vapour_extinction_rate,
        planck_over_wavelength,
        layer_sightline_position,
        thermal_field,
        particulate_fraction,
        picture_adjoint_seed.reshape(2 * NB, COLS * LANES),
    )
    return (
        radiance.reshape(NB, 2, COLS * LANES),
        gradient - quot.reshape(1, LINES, LANES),
    )


def solution(mesh):
    placed = (
        P("depth", None, "width"),
        P("depth", None, "width"),
        P(),
        P(),
        P(),
        P(),
        P(None, ("depth", "width"), None),
    )
    return jax.shard_map(
        on_device,
        mesh=mesh,
        in_specs=placed,
        out_specs=(P(None, ("depth", "width"), None), P("depth", None, "width")),
        check_vma=False,
    )
```

time: 103 us -> 50.9 us (0.49)
  waiting for transfers between devices: 39 us -> 0 us
  starting transfers between devices: 27.4 us -> 0 us
  Pallas kernels: 24.3 us -> 43.8 us
  local copies, waits for them, and re-layouts: 9.78 us -> 3.28 us
  other arithmetic: 1.34 us -> 3.08 us
    all_to_all x4 -> x0, waiting for transfers between devices: 39 us -> none  [the longest x1 17.7 us: on_device(): lax.all_to_all(sent.reshape(NB + 2, SLABS, ROWS, LANES), 'depth', split_a...]
    all_to_all x4 -> x0, starting transfers between devices: 27.4 us -> none  [the longest x1 8.59 us: on_device(): lax.all_to_all(picture_adjoint_seed.reshape(NB, 2, 16, LANES), 'width', s...]
    pallas_call x3 -> x1, Pallas kernels: 24.3 us -> 43.8 us  [on_device(): pl.pallas_call(kernel, out_shape=(jax.ShapeDtypeStruct((2 * NB, COLS * LA...]
    unnamed x12 -> x0, local copies, waits for them, and re-layouts: 3.73 us -> none
    sub x0 -> x1, other arithmetic: none -> 3.08 us  [on_device(): gradient - quot.reshape(1, LINES, LANES)]
    all_to_all x4 -> x0, local copies, waits for them, and re-layouts: 1.58 us -> none  [the longest x1 1.37 us: on_device(): lax.all_to_all(back, 'depth', split_axis=1, concat_axis=1, tiled=True)]
    another operation x2 -> x0, other arithmetic: 1.34 us -> none  [on_device(): jnp.stack([sootiness_extinction * (-LOG2E / CD), vapour_extinction_rate *...]
    pallas_call x1 -> x0, local copies, waits for them, and re-layouts: 1.1 us -> none  [on_device(): pl.pallas_call(compose_kernel, out_shape=(jax.ShapeDtypeStruct((NB, ROWS,...]
  transfers between devices with their start and end apart: 4 -> 0, of which waited for: 3 -> 0; matrix products, arithmetic and copies ran while one was open for 4% -> 0% of each run, Pallas kernels for 8% -> 0%
where the time goes in v1:
time: 50.9 us; the launch traced here: 50.8 us
  Pallas kernels  43.8 us (86%)
  local copies, waits for them, and re-layouts  3.28 us (6%)
  other arithmetic  3.08 us (6%)
  between operations  0.64 us (1%)
    pallas_call x1, Pallas kernels, on_device(): pl.pallas_call(kernel, out_shape=(jax.ShapeDtypeStruct((2 * NB, COLS * LA...  43.8 us
    sub x1, other arithmetic, on_device(): gradient - quot.reshape(1, LINES, LANES)  3.08 us
    reshape x1, local copies, waits for them, and re-layouts, on_device(): picture_adjoint_seed.reshape(2 * NB, COLS * LANES)  1.65 us
    reshape x1, local copies, waits for them, and re-layouts, on_device(): radiance.reshape(NB, 2, COLS * LANES)  1.63 us

profile of v1, /device:TPU:1, one launch (start us, length us, event | category | flops | bytes accessed | tf_op | source)
XLA Modules:
  0.0 50.8 jit_solution(6456093925689140586)
XLA Ops:
  0.6 1.6 %reshape.12.seed_hbm = f32[16,2048]{1,0:T(8,128)} reshape(f32[8,2,2048]{2,1,0:T(2,128)} %param.13) | data formatting | bytes 262144 | tf_op jit(solution)/shard_map/reshape | solution.py:545
  2.3 43.8 %shard_map.86 = (f32[16,2048]{1,0:T(8,128)}, f32[16,256,128]{2,1,0:T(8,128)}, f32[8,32,128]{2,1,0:T(8,128)}) custom-call(f32[8]{0:T(128)} %soot.1, f32[8]{0:T(128)} %vapour.1, f32[8]{0:T(128)} %planck.1, s32[8]{0:T(128)} %pos.1, f32[16,256,128]{2,1,0:T(8,128)} %t_hbm.1, bf16[16,256,128]{2,1,0:T(8,128)(2,1)} %p_hbm.1, f32[16,2048]{1,0:T(8,128)} %reshape.12.seed_hbm), custom_call_target="tpu_custom_call" | custom-call | tf_op jit(solution)/shard_map/pallas_call | solution.py:479
  46.1 1.6 %reshape.13 = f32[8,2,2048]{2,1,0:T(2,128)} reshape(f32[16,2048]{1,0:T(8,128)} %get-tuple-element.5) | data formatting | bytes 262144 | tf_op jit(solution)/shard_map/reshape | solution.py:548
  47.7 3.1 %broadcast_subtract_fusion = f32[16,256,128]{2,1,0:T(8,128)} fusion(f32[16,256,128]{2,1,0:T(8,128)} %get-tuple-element.6, f32[256,128]{1,0:T(8,128)} %bitcast.1), kind=kLoop, calls=%fused_computation | loop fusion | flops 524288 | bytes 4325376 | tf_op jit(solution)/shard_map/sub | solution.py:549

commit v2 on v1

--- a/solution.py
+++ b/solution.py
@@ -131,21 +131,15 @@
         table[1, b] = scale * gas[b]
         table[2, b] = jnp.full(TILE, planck[b], F32) / gas[b]
 
-    pl.semaphore_wait(barrier, SLABS + COLS - 2)
-
     def cols(i):
         return pl.ds(pl.multiple_of(i * LANES, LANES), LANES)
 
     def seed_copy(to, slot):
         return rdma(
-            seed_hbm.at[:, cols(to)], seed_l.at[slot], seed_ss.at[to], seed_rs.at[slot], {"width": to}
-        )
-
-    @pl.loop(1, COLS)
-    def _(o):
-        seed_copy(lax.rem(w + o, COLS), w).start()
-
-    seed_own = pltpu.make_async_copy(seed_hbm.at[:, cols(w)], seed_l.at[w], out_sem.at[SLABS])
+            seed_hbm.at[:, :, cols(to)], seed_l.at[slot], seed_ss.at[to], seed_rs.at[slot], {"width": to}
+        )
+
+    seed_own = pltpu.make_async_copy(seed_hbm.at[:, :, cols(w)], seed_l.at[w], out_sem.at[SLABS])
     seed_own.start()
 
     def exchange(send, recv, ss, rs):
@@ -186,8 +180,6 @@
                     sum_s[e, 0, pl.ds(r16, 16), :] = pp
                     sum_s[e, 1, pl.ds(r16, 16), :] = tt
 
-            if not (i == CHIPS - 1 and half == 1):
-                sums(e, d).start()
 
     def heavy(n0, n1):
         @pl.loop(n0, n1)
@@ -262,7 +254,7 @@
             for r in range(2):
                 for h in range(2):
                     seed_a[d, pl.ds(ROWS * b + r + 16 * h, 8, stride=2), :] = seed_l[
-                        pl.ds(8 * h, 8), 2 * b + r, :
+                        pl.ds(8 * h, 8), b, r, :
                     ]
         for i in (2, 1, 3):
             sax(same(i), d).start()
@@ -278,14 +270,15 @@
         tt = fro_r[e, 1, pl.ds(r8, 8), :]
         return [jnp.exp2(ks[b] * pp + kv[b] * tt) for b in range(NB)]
 
-    def fade(n0, n1):
-        @pl.loop(n0, n1)
-        def _(n):
-            e, r8 = tile_of(n)
-            dim = dims(e, r8)
-            for b in range(NB):
-                rows = pl.ds(ROWS * b + r8, 8)
-                lit[e, rows, :] = lit[e, rows, :] * dim[b]
+    def fade(g0, g1):
+        @pl.loop(g0, g1)
+        def _(g):
+            e, _ = tile_of(4 * g)
+            for j in range(4):
+                dim = dims(e, 8 * j)
+                for b in range(NB):
+                    rows = pl.ds(ROWS * b + 8 * j, 8)
+                    lit[e, rows, :] = lit[e, rows, :] * dim[b]
 
     def pairs(i, slot):
         return rdma(
@@ -305,41 +298,44 @@
         pairs(i, chip(i)).wait_recv()
         e = 2 * chip(i) + c
 
-        @pl.loop(0, NB * ROWS // 8)
+        @pl.loop(0, 4)
         def _(j):
-            rows = pl.ds(pl.multiple_of(8 * j, 8), 8)
+            rows = pl.ds(pl.multiple_of(64 * j, 64), 64)
             chip_s[i, rows, :] = lit[e, rows, :] + pair_r[chip(i), rows, :]
 
-    heavy(0, 12)
+    heavy(0, 4)
+    pl.semaphore_wait(barrier, SLABS + COLS - 2)
+    for p in others():
+        sums(p, d).start()
+
+    @pl.loop(1, COLS)
+    def _(o):
+        seed_copy(lax.rem(w + o, COLS), w).start()
+
+    heavy(4, 16)
     make_fronts()
-    heavy(12, 16)
     spread_seeds()
-    heavy(16, 24)
-    forward_seeds()
+    heavy(16, 32)
     for p in others():
         fronts(p, p).wait_recv()
-    for i in range(3):
-        fade(8 * i, 8 * i + 8)
+    for i in range(CHIPS):
+        fade(2 * i, 2 * i + 2)
         pairs(i, chip(i)).start()
-    heavy(24, 28)
     for i in range(3):
         join(i)
         chips(i, x).start()
-    heavy(28, 32)
-    fade(24, 32)
-    pairs(3, chip(3)).start()
-
+    forward_seeds()
     for s in range(CHIPS):
         sap(2 * s + 1 - c).wait_recv()
 
-    @pl.loop(0, 32)
-    def _(n):
-        e, r8 = tile_of(n)
-        total = jnp.zeros(TILE, F32)
-        for b in range(NB):
-            rows = pl.ds(ROWS * b + r8, 8)
-            total = total + gas[b] * (seed_a[e, rows, :] * lit[e, rows, :])
-        gs_s[e, pl.ds(r8, 8), :] = total
+    @pl.loop(0, SLABS)
+    def _(e):
+        for j in range(4):
+            total = gas[0] * (seed_a[e, pl.ds(8 * j, 8), :] * lit[e, pl.ds(8 * j, 8), :])
+            for b in range(1, NB):
+                rows = pl.ds(ROWS * b + 8 * j, 8)
+                total = total + gas[b] * (seed_a[e, rows, :] * lit[e, rows, :])
+            gs_s[e, pl.ds(8 * j, 8), :] = total
 
     gs_r[d] = gs_s[d]
     for p in others():
@@ -372,15 +368,15 @@
 
             out_copy(g).start()
 
-    finish(0, 4)
+    finish(0, SLABS)
 
     pairs(3, x).wait_recv()
     for i in range(3):
         chips(i, chip(i)).wait_recv()
 
-    @pl.loop(0, NB * ROWS // 8)
+    @pl.loop(0, 4)
     def _(j):
-        rows = pl.ds(pl.multiple_of(8 * j, 8), 8)
+        rows = pl.ds(pl.multiple_of(64 * j, 64), 64)
         rad_v[rows, :] = (
             (lit[d, rows, :] + pair_r[x, rows, :])
             + (chip_r[chip(0), rows, :] + chip_r[chip(1), rows, :])
@@ -390,14 +386,14 @@
     for b in range(NB):
         for r in range(2):
             for h in range(2):
-                rad_s[pl.ds(8 * h, 8), 2 * b + r, :] = rad_v[
+                rad_s[pl.ds(8 * h, 8), b, r, :] = rad_v[
                     pl.ds(ROWS * b + r + 16 * h, 8, stride=2), :
                 ]
-    rad_r[:, cols(w)] = rad_s[w]
+    rad_r[:, :, cols(w)] = rad_s[w]
 
     def rad_copy(to, slot):
         return rdma(
-            rad_s.at[to], rad_r.at[:, cols(slot)], rad_ss.at[to], rad_rs.at[slot], {"width": to}
+            rad_s.at[to], rad_r.at[:, :, cols(slot)], rad_ss.at[to], rad_rs.at[slot], {"width": to}
         )
 
     @pl.loop(1, COLS)
@@ -421,7 +417,6 @@
     q_r[d] = q_s[d]
     for p in others():
         quots(p, d).start()
-    finish(4, 8)
 
     for p in others():
         quots(p, p).wait_recv()
@@ -453,6 +448,12 @@
         p = lax.rem(w + o, COLS)
         seed_copy(p, w).wait_send()
         rad_copy(p, w).wait_send()
+
+
+def subtract_kernel(g_ref, q_ref, o_ref):
+    q = q_ref[...]
+    for k in range(CD):
+        o_ref[k] = g_ref[k] - q
 
 
 def on_device(
@@ -479,7 +480,7 @@
     radiance, gradient, quot = pl.pallas_call(
         kernel,
         out_shape=(
-            jax.ShapeDtypeStruct((2 * NB, COLS * LANES), F32),
+            jax.ShapeDtypeStruct((NB, 2, COLS * LANES), F32),
             jax.ShapeDtypeStruct(field, F32),
             jax.ShapeDtypeStruct((SLABS, ROWS, LANES), F32),
         ),
@@ -495,7 +496,7 @@
             v(SLABS, 2, ROWS, LANES),
             v(SLABS, 2, ROWS, LANES),
             v(SLABS, 2, ROWS, LANES),
-            v(COLS, 2 * NB, LANES),
+            v(COLS, NB, 2, LANES),
             v(SLABS, *image),
             v(SLABS, *image),
             v(CHIPS, *image),
@@ -506,8 +507,8 @@
             v(SLABS, ROWS, LANES),
             v(SLABS, ROWS, LANES),
             v(*image),
-            v(COLS, 2 * NB, LANES),
-            v(2 * NB, COLS * LANES),
+            v(COLS, NB, 2, LANES),
+            v(NB, 2, COLS * LANES),
             v(*field),
             sems(2, CHIPS),
             sems(SLABS + 1),
@@ -542,12 +543,17 @@
         layer_sightline_position,
         thermal_field,
         particulate_fraction,
-        picture_adjoint_seed.reshape(2 * NB, COLS * LANES),
+        picture_adjoint_seed,
     )
-    return (
-        radiance.reshape(NB, 2, COLS * LANES),
-        gradient - quot.reshape(1, LINES, LANES),
-    )
+    cells = pl.BlockSpec((CD, 2 * ROWS, LANES), lambda i: (0, i, 0))
+    gradient = pl.pallas_call(
+        subtract_kernel,
+        grid=(LINES // (2 * ROWS),),
+        out_shape=jax.ShapeDtypeStruct(field, F32),
+        in_specs=[cells, pl.BlockSpec((2 * ROWS, LANES), lambda i: (i, 0))],
+        out_specs=cells,
+    )(gradient, quot.reshape(LINES, LANES))
+    return radiance, gradient
 
 
 def solution(mesh):

time: 50.9 us -> 45.2 us (0.89)
  other arithmetic: 3.08 us -> 0 us
  local copies, waits for them, and re-layouts: 3.28 us -> 0.66 us
    reshape x2 -> x0, local copies, waits for them, and re-layouts: 3.28 us -> none  [the longest x1 1.65 us: on_device(): picture_adjoint_seed.reshape(2 * NB, COLS * LANES)]
    sub x1 -> x0, other arithmetic: 3.08 us -> none  [on_device(): gradient - quot.reshape(1, LINES, LANES)]
    unnamed x0 -> x3, local copies, waits for them, and re-layouts: none -> 0.66 us
    pallas_call x1 -> x2, Pallas kernels: 43.8 us -> 43.7 us  [the longest x1 39.9 us: on_device(): pl.pallas_call(kernel, out_shape=(jax.ShapeDtypeStruct((NB, 2, COLS * LAN...]
where the time goes in v2:
time: 45.2 us; the launch traced here: 45 us
  Pallas kernels  43.7 us (97%)
  local copies, waits for them, and re-layouts  0.66 us (1%)
  between operations  0.65 us (1%)
    pallas_call x1, Pallas kernels, on_device(): pl.pallas_call(kernel, out_shape=(jax.ShapeDtypeStruct((NB, 2, COLS * LAN...  39.9 us
    pallas_call x1, Pallas kernels, on_device(): pl.pallas_call(subtract_kernel, grid=(LINES // (2 * ROWS),), out_shape=ja...  3.84 us

profile of v2, /device:TPU:1, one launch (start us, length us, event | category | flops | bytes accessed | tf_op | source)
XLA Modules:
  0.0 45.0 jit_solution(678795876264438869)
XLA Ops:
  0.6 39.9 %shard_map.86 = (f32[8,2,2048]{2,1,0:T(2,128)}, f32[16,256,128]{2,1,0:T(8,128)}, f32[8,32,128]{2,1,0:T(8,128)}) custom-call(f32[8]{0:T(128)} %soot.1, f32[8]{0:T(128)} %vapour.1, f32[8]{0:T(128)} %planck.1, s32[8]{0:T(128)} %pos.1, f32[16,256,128]{2,1,0:T(8,128)} %t_hbm.1, bf16[16,256,128]{2,1,0:T(8,128)(2,1)} %p_hbm.1, f32[8,2,2048]{2,1,0:T(2,128)} %seed_hbm.1), custom_call_target="tpu_custom_call" | custom-call | tf_op jit(solution)/shard_map/pallas_call | solution.py:480
  40.5 0.0 copy-start
  40.5 3.8 %shard_map.87 = f32[16,256,128]{2,1,0:T(8,128)} custom-call(f32[16,256,128]{2,1,0:T(8,128)} %get-tuple-element.6.g_ref, f32[256,128]{1,0:T(8,128)} %bitcast.1), custom_call_target="tpu_custom_call" | custom-call | tf_op jit(solution)/shard_map/pallas_call | solution.py:549
  44.4 0.0 copy-done
  44.4 0.7 %copy.10 = f32[8,2,2048]{2,1,0:T(2,128)} copy(f32[8,2,2048]{2,1,0:T(2,128)S(1)} %copy-done) | data formatting | bytes 262144
Async XLA Ops:
  40.5 3.9 %copy-start = (f32[8,2,2048]{2,1,0:T(2,128)S(1)}, f32[8,2,2048]{2,1,0:T(2,128)}, u32[]{:S(2)}) copy-start(f32[8,2,2048]{2,1,0:T(2,128)} %get-tuple-element.10) | copy-start | bytes 393220

commit v3 on v2

--- a/solution.py
+++ b/solution.py
@@ -30,7 +30,7 @@
     p_hbm,
     seed_hbm,
     rad_out,
-    grad_hbm,
+    grad_v,
     q_out,
     t_v,
     p_v,
@@ -54,7 +54,6 @@
     rad_v,
     rad_s,
     rad_r,
-    grad_v,
     in_sem,
     out_sem,
     sum_ss,
@@ -141,6 +140,11 @@
 
     seed_own = pltpu.make_async_copy(seed_hbm.at[:, :, cols(w)], seed_l.at[w], out_sem.at[SLABS])
     seed_own.start()
+    pl.semaphore_wait(barrier, SLABS + COLS - 2)
+
+    @pl.loop(1, COLS)
+    def _(o):
+        seed_copy(lax.rem(w + o, COLS), w).start()
 
     def exchange(send, recv, ss, rs):
         def make(to, slot):
@@ -179,6 +183,9 @@
                 else:
                     sum_s[e, 0, pl.ds(r16, 16), :] = pp
                     sum_s[e, 1, pl.ds(r16, 16), :] = tt
+
+            if not (i == CHIPS - 1 and half == 1):
+                sums(e, d).start()
 
 
     def heavy(n0, n1):
@@ -303,27 +310,24 @@
             rows = pl.ds(pl.multiple_of(64 * j, 64), 64)
             chip_s[i, rows, :] = lit[e, rows, :] + pair_r[chip(i), rows, :]
 
-    heavy(0, 4)
-    pl.semaphore_wait(barrier, SLABS + COLS - 2)
-    for p in others():
-        sums(p, d).start()
-
-    @pl.loop(1, COLS)
-    def _(o):
-        seed_copy(lax.rem(w + o, COLS), w).start()
-
-    heavy(4, 16)
+    heavy(0, 12)
     make_fronts()
+    heavy(12, 20)
     spread_seeds()
-    heavy(16, 32)
+    heavy(20, 24)
     for p in others():
         fronts(p, p).wait_recv()
-    for i in range(CHIPS):
+    for i in range(3):
         fade(2 * i, 2 * i + 2)
         pairs(i, chip(i)).start()
+    heavy(24, 28)
+    fade(6, 7)
+    pairs(3, chip(3)).start()
     for i in range(3):
         join(i)
         chips(i, x).start()
+    heavy(28, 32)
+    fade(7, 8)
     forward_seeds()
     for s in range(CHIPS):
         sap(2 * s + 1 - c).wait_recv()
@@ -340,13 +344,6 @@
     gs_r[d] = gs_s[d]
     for p in others():
         grads(p, d).start()
-
-    def out_copy(g):
-        e, _ = tile_of(4 * g)
-        rows = pl.ds(pl.multiple_of(ROWS * e, ROWS), ROWS)
-        return pltpu.make_async_copy(
-            grad_v.at[:, rows, :], grad_hbm.at[:, rows, :], out_sem.at[g]
-        )
 
     def finish(g0, g1):
         @pl.loop(g0, g1)
@@ -366,7 +363,6 @@
                         acc = acc + wt[b] * big[b, k, rows, :]
                     grad_v[k, rows, :] = acc
 
-            out_copy(g).start()
 
     finish(0, SLABS)
 
@@ -428,8 +424,6 @@
         rad_copy(p, p).wait_recv()
 
     rad_out[...] = rad_r[...]
-    for g in range(SLABS):
-        out_copy(g).wait()
     for p in others():
         sums(p, d).wait_send()
         fronts(p, d).wait_send()
@@ -450,10 +444,21 @@
         rad_copy(p, w).wait_send()
 
 
-def subtract_kernel(g_ref, q_ref, o_ref):
-    q = q_ref[...]
+def subtract_kernel(q_ref, g_ref, r_ref, o_hbm, rad_hbm, buf, out_sem):
+    picture = pltpu.make_async_copy(r_ref, rad_hbm, out_sem.at[CD])
+    picture.start()
+
+    def store(k):
+        return pltpu.make_async_copy(buf.at[k], o_hbm.at[k], out_sem.at[k])
+
     for k in range(CD):
-        o_ref[k] = g_ref[k] - q
+        for e in range(SLABS):
+            rows = pl.ds(ROWS * e, ROWS)
+            buf[k, rows, :] = g_ref[k, rows, :] - q_ref[e]
+        store(k).start()
+    for k in range(CD):
+        store(k).wait()
+    picture.wait()
 
 
 def on_device(
@@ -480,12 +485,12 @@
     radiance, gradient, quot = pl.pallas_call(
         kernel,
         out_shape=(
-            jax.ShapeDtypeStruct((NB, 2, COLS * LANES), F32),
-            jax.ShapeDtypeStruct(field, F32),
-            jax.ShapeDtypeStruct((SLABS, ROWS, LANES), F32),
+            pltpu.VMEM((NB, 2, COLS * LANES), F32),
+            pltpu.VMEM(field, F32),
+            pltpu.VMEM((SLABS, ROWS, LANES), F32),
         ),
         in_specs=[smem, smem, smem, smem, hbm, hbm, hbm],
-        out_specs=(vmem, hbm, vmem),
+        out_specs=(vmem, vmem, vmem),
         scratch_shapes=[
             v(*field),
             pltpu.VMEM(field, jnp.bfloat16),
@@ -509,7 +514,6 @@
             v(*image),
             v(COLS, NB, 2, LANES),
             v(NB, 2, COLS * LANES),
-            v(*field),
             sems(2, CHIPS),
             sems(SLABS + 1),
             sems(SLABS),
@@ -545,14 +549,17 @@
         particulate_fraction,
         picture_adjoint_seed,
     )
-    cells = pl.BlockSpec((CD, 2 * ROWS, LANES), lambda i: (0, i, 0))
-    gradient = pl.pallas_call(
+    gradient, radiance = pl.pallas_call(
         subtract_kernel,
-        grid=(LINES // (2 * ROWS),),
-        out_shape=jax.ShapeDtypeStruct(field, F32),
-        in_specs=[cells, pl.BlockSpec((2 * ROWS, LANES), lambda i: (i, 0))],
-        out_specs=cells,
-    )(gradient, quot.reshape(LINES, LANES))
+        out_shape=(
+            jax.ShapeDtypeStruct(field, F32),
+            jax.ShapeDtypeStruct((NB, 2, COLS * LANES), F32),
+        ),
+        in_specs=[vmem, vmem, vmem],
+        out_specs=(hbm, hbm),
+        scratch_shapes=[v(*field), sems(CD + 1)],
+        compiler_params=pltpu.CompilerParams(vmem_limit_bytes=8 << 20),
+    )(quot, gradient, radiance)
     return radiance, gradient
 
 

time: 45.2 us -> 41.2 us (0.912)
  Pallas kernels: 43.7 us -> 40.4 us
  local copies, waits for them, and re-layouts: 0.66 us -> 0 us
    pallas_call x2, Pallas kernels: 43.7 us -> 40.4 us  [the longest x1 38.9 us: on_device(): pl.pallas_call(kernel, out_shape=(pltpu.VMEM((NB, 2, COLS * LANES), F32),...]
    unnamed x3 -> x0, local copies, waits for them, and re-layouts: 0.66 us -> none
where the time goes in v3:
time: 41.2 us; the launch traced here: 41.1 us
  Pallas kernels  40.4 us (98%)
  between operations  0.64 us (2%)
    pallas_call x1, Pallas kernels, on_device(): pl.pallas_call(kernel, out_shape=(pltpu.VMEM((NB, 2, COLS * LANES), F32),...  38.9 us
    pallas_call x1, Pallas kernels, on_device(): pl.pallas_call(subtract_kernel, out_shape=(jax.ShapeDtypeStruct(field, F3...  1.49 us

profile of v3, /device:TPU:1, one launch (start us, length us, event | category | flops | bytes accessed | tf_op | source)
XLA Modules:
  0.0 41.1 jit_solution(9527989308637614341)
XLA Ops:
  0.6 38.9 %shard_map.86 = (f32[8,2,2048]{2,1,0:T(2,128)S(1)}, f32[16,256,128]{2,1,0:T(8,128)S(1)}, f32[8,32,128]{2,1,0:T(8,128)S(1)}) custom-call(f32[8]{0:T(128)} %soot.1, f32[8]{0:T(128)} %vapour.1, f32[8]{0:T(128)} %planck.1, s32[8]{0:T(128)} %pos.1, f32[16,256,128]{2,1,0:T(8,128)} %t_hbm.1, bf16[16,256,128]{2,1,0:T(8,128)(2,1)} %p_hbm.1, f32[8,2,2048]{2,1,0:T(2,128)} %seed_hbm.1), custom_call_target="tpu_custom_call" | custom-call | tf_op jit(solution)/shard_map/pallas_call | solution.py:485
  39.6 1.5 %shard_map.87 = (f32[16,256,128]{2,1,0:T(8,128)}, f32[8,2,2048]{2,1,0:T(2,128)}) custom-call(f32[8,32,128]{2,1,0:T(8,128)S(1)} %get-tuple-element.7.q_ref, f32[16,256,128]{2,1,0:T(8,128)S(1)} %get-tuple-element.8.g_ref, f32[8,2,2048]{2,1,0:T(2,128)S(1)} %get-tuple-element.9.r_ref), custom_call_target="tpu_custom_call" | custom-call | tf_op jit(solution)/shard_map/pallas_call | solution.py:552

commit v4 on v3

--- a/solution.py
+++ b/solution.py
@@ -312,22 +312,21 @@
 
     heavy(0, 12)
     make_fronts()
-    heavy(12, 20)
+    heavy(12, 16)
     spread_seeds()
-    heavy(20, 24)
+    heavy(16, 24)
     for p in others():
         fronts(p, p).wait_recv()
     for i in range(3):
         fade(2 * i, 2 * i + 2)
         pairs(i, chip(i)).start()
-    heavy(24, 28)
-    fade(6, 7)
-    pairs(3, chip(3)).start()
+    heavy(24, 26)
     for i in range(3):
         join(i)
         chips(i, x).start()
-    heavy(28, 32)
-    fade(7, 8)
+    heavy(26, 32)
+    fade(6, 8)
+    pairs(3, chip(3)).start()
     forward_seeds()
     for s in range(CHIPS):
         sap(2 * s + 1 - c).wait_recv()

time: 41.2 us -> 41.2 us (level)
  no operation moved by 1% of the time
where the time goes in v4:
time: 41.2 us; the launch traced here: 41.1 us
  Pallas kernels  40.4 us (98%)
  between operations  0.64 us (2%)
    pallas_call x1, Pallas kernels, on_device(): pl.pallas_call(kernel, out_shape=(pltpu.VMEM((NB, 2, COLS * LANES), F32),...  38.9 us
    pallas_call x1, Pallas kernels, on_device(): pl.pallas_call(subtract_kernel, out_shape=(jax.ShapeDtypeStruct(field, F3...  1.49 us

profile of v4, /device:TPU:1, one launch (start us, length us, event | category | flops | bytes accessed | tf_op | source)
XLA Modules:
  0.0 41.1 jit_solution(13801334097428067808)
XLA Ops:
  0.6 38.9 %shard_map.86 = (f32[8,2,2048]{2,1,0:T(2,128)S(1)}, f32[16,256,128]{2,1,0:T(8,128)S(1)}, f32[8,32,128]{2,1,0:T(8,128)S(1)}) custom-call(f32[8]{0:T(128)} %soot.1, f32[8]{0:T(128)} %vapour.1, f32[8]{0:T(128)} %planck.1, s32[8]{0:T(128)} %pos.1, f32[16,256,128]{2,1,0:T(8,128)} %t_hbm.1, bf16[16,256,128]{2,1,0:T(8,128)(2,1)} %p_hbm.1, f32[8,2,2048]{2,1,0:T(2,128)} %seed_hbm.1), custom_call_target="tpu_custom_call" | custom-call | tf_op jit(solution)/shard_map/pallas_call | solution.py:484
  39.6 1.5 %shard_map.87 = (f32[16,256,128]{2,1,0:T(8,128)}, f32[8,2,2048]{2,1,0:T(2,128)}) custom-call(f32[8,32,128]{2,1,0:T(8,128)S(1)} %get-tuple-element.7.q_ref, f32[16,256,128]{2,1,0:T(8,128)S(1)} %get-tuple-element.8.g_ref, f32[8,2,2048]{2,1,0:T(2,128)S(1)} %get-tuple-element.9.r_ref), custom_call_target="tpu_custom_call" | custom-call | tf_op jit(solution)/shard_map/pallas_call | solution.py:551

commit v5 on v4

--- a/solution.py
+++ b/solution.py
@@ -142,9 +142,13 @@
     seed_own.start()
     pl.semaphore_wait(barrier, SLABS + COLS - 2)
 
-    @pl.loop(1, COLS)
-    def _(o):
-        seed_copy(lax.rem(w + o, COLS), w).start()
+    steps = sorted(
+        ((a, b) for a in range(4) for b in range(4) if a or b),
+        key=lambda s: -(min(s[0], 4 - s[0]) + min(s[1], 4 - s[1])),
+    )
+    across = [4 * lax.rem(w // 4 + a, 4) + lax.rem(lax.rem(w, 4) + b, 4) for a, b in steps]
+    for p in across:
+        seed_copy(p, w).start()
 
     def exchange(send, recv, ss, rs):
         def make(to, slot):
@@ -391,9 +395,8 @@
             rad_s.at[to], rad_r.at[:, :, cols(slot)], rad_ss.at[to], rad_rs.at[slot], {"width": to}
         )
 
-    @pl.loop(1, COLS)
-    def _(o):
-        rad_copy(lax.rem(w + o, COLS), w).start()
+    for p in across:
+        rad_copy(p, w).start()
 
     for p in others():
         grads(p, p).wait_recv()

time: 41.2 us -> 41.1 us (level)
  no operation moved by 1% of the time
where the time goes in v5:
time: 41.1 us; the launch traced here: 41 us
  Pallas kernels  40.3 us (98%)
  between operations  0.64 us (2%)
    pallas_call x1, Pallas kernels, on_device(): pl.pallas_call(kernel, out_shape=(pltpu.VMEM((NB, 2, COLS * LANES), F32),...  38.8 us
    pallas_call x1, Pallas kernels, on_device(): pl.pallas_call(subtract_kernel, out_shape=(jax.ShapeDtypeStruct(field, F3...  1.49 us

profile of v5, /device:TPU:1, one launch (start us, length us, event | category | flops | bytes accessed | tf_op | source)
XLA Modules:
  0.0 41.0 jit_solution(6420202676079060757)
XLA Ops:
  0.6 38.8 %shard_map.86 = (f32[8,2,2048]{2,1,0:T(2,128)S(1)}, f32[16,256,128]{2,1,0:T(8,128)S(1)}, f32[8,32,128]{2,1,0:T(8,128)S(1)}) custom-call(f32[8]{0:T(128)} %soot.1, f32[8]{0:T(128)} %vapour.1, f32[8]{0:T(128)} %planck.1, s32[8]{0:T(128)} %pos.1, f32[16,256,128]{2,1,0:T(8,128)} %t_hbm.1, bf16[16,256,128]{2,1,0:T(8,128)(2,1)} %p_hbm.1, f32[8,2,2048]{2,1,0:T(2,128)} %seed_hbm.1), custom_call_target="tpu_custom_call" | custom-call | tf_op jit(solution)/shard_map/pallas_call | solution.py:487
  39.5 1.5 %shard_map.87 = (f32[16,256,128]{2,1,0:T(8,128)}, f32[8,2,2048]{2,1,0:T(2,128)}) custom-call(f32[8,32,128]{2,1,0:T(8,128)S(1)} %get-tuple-element.7.q_ref, f32[16,256,128]{2,1,0:T(8,128)S(1)} %get-tuple-element.8.g_ref, f32[8,2,2048]{2,1,0:T(2,128)S(1)} %get-tuple-element.9.r_ref), custom_call_target="tpu_custom_call" | custom-call | tf_op jit(solution)/shard_map/pallas_call | solution.py:554

commit v6 on v3

--- a/solution.py
+++ b/solution.py
@@ -240,14 +240,16 @@
     def same(i):
         return lax.rem(d + 2 * i, SLABS)
 
-    def sax(to, slot):
+    def sax(to, slot, h):
+        part = seed_a.at[slot, pl.ds(NB * ROWS // 2 * h, NB * ROWS // 2)]
         return rdma(
-            seed_a.at[slot], seed_a.at[slot], sax_ss.at[to // 2], sax_rs.at[slot // 2], {"depth": to}
-        )
-
-    def sap(slot):
+            part, part, sax_ss.at[2 * (to // 2) + h], sax_rs.at[2 * (slot // 2) + h], {"depth": to}
+        )
+
+    def sap(slot, h):
+        part = seed_a.at[slot, pl.ds(NB * ROWS // 2 * h, NB * ROWS // 2)]
         return rdma(
-            seed_a.at[slot], seed_a.at[slot], sap_ss.at[slot // 2], sap_rs.at[slot // 2], {"depth": pair}
+            part, part, sap_ss.at[2 * (slot // 2) + h], sap_rs.at[2 * (slot // 2) + h], {"depth": pair}
         )
 
     def spread_seeds():
@@ -263,14 +265,17 @@
                     seed_a[d, pl.ds(ROWS * b + r + 16 * h, 8, stride=2), :] = seed_l[
                         pl.ds(8 * h, 8), b, r, :
                     ]
+
+    def send_seeds(h):
         for i in (2, 1, 3):
-            sax(same(i), d).start()
-        sap(d).start()
+            sax(same(i), d, h).start()
+        sap(d, h).start()
 
     def forward_seeds():
-        for i in (1, 3, 2):
-            sax(same(i), same(i)).wait_recv()
-            sap(same(i)).start()
+        for h in range(2):
+            for i in (1, 3, 2):
+                sax(same(i), same(i), h).wait_recv()
+                sap(same(i), h).start()
 
     def dims(e, r8):
         pp = fro_r[e, 0, pl.ds(r8, 8), :]
@@ -312,8 +317,10 @@
 
     heavy(0, 12)
     make_fronts()
+    spread_seeds()
+    send_seeds(0)
     heavy(12, 20)
-    spread_seeds()
+    send_seeds(1)
     heavy(20, 24)
     for p in others():
         fronts(p, p).wait_recv()
@@ -330,7 +337,8 @@
     fade(7, 8)
     forward_seeds()
     for s in range(CHIPS):
-        sap(2 * s + 1 - c).wait_recv()
+        for h in range(2):
+            sap(2 * s + 1 - c, h).wait_recv()
 
     @pl.loop(0, SLABS)
     def _(e):
@@ -430,9 +438,11 @@
         grads(p, d).wait_send()
         quots(p, d).wait_send()
     for i in (1, 2, 3):
-        sax(same(i), d).wait_send()
+        for h in range(2):
+            sax(same(i), d, h).wait_send()
     for s in range(CHIPS):
-        sap(2 * s + c).wait_send()
+        for h in range(2):
+            sap(2 * s + c, h).wait_send()
         pairs(s, chip(s)).wait_send()
     for i in range(3):
         chips(i, x).wait_send()
@@ -522,10 +532,10 @@
             sems(SLABS),
             sems(COLS),
             sems(COLS),
-            sems(CHIPS),
-            sems(CHIPS),
-            sems(CHIPS),
-            sems(CHIPS),
+            sems(SLABS),
+            sems(SLABS),
+            sems(SLABS),
+            sems(SLABS),
             sems(CHIPS),
             sems(CHIPS),
             sems(3),

time: 41.2 us -> 41.1 us (level)
  no operation moved by 1% of the time
where the time goes in v6:
time: 41.1 us; the launch traced here: 41 us
  Pallas kernels  40.4 us (98%)
  between operations  0.64 us (2%)
    pallas_call x1, Pallas kernels, on_device(): pl.pallas_call(kernel, out_shape=(pltpu.VMEM((NB, 2, COLS * LANES), F32),...  38.9 us
    pallas_call x1, Pallas kernels, on_device(): pl.pallas_call(subtract_kernel, out_shape=(jax.ShapeDtypeStruct(field, F3...  1.49 us

profile of v6, /device:TPU:1, one launch (start us, length us, event | category | flops | bytes accessed | tf_op | source)
XLA Modules:
  0.0 41.0 jit_solution(6745459261331837282)
XLA Ops:
  0.6 38.9 %shard_map.86 = (f32[8,2,2048]{2,1,0:T(2,128)S(1)}, f32[16,256,128]{2,1,0:T(8,128)S(1)}, f32[8,32,128]{2,1,0:T(8,128)S(1)}) custom-call(f32[8]{0:T(128)} %soot.1, f32[8]{0:T(128)} %vapour.1, f32[8]{0:T(128)} %planck.1, s32[8]{0:T(128)} %pos.1, f32[16,256,128]{2,1,0:T(8,128)} %t_hbm.1, bf16[16,256,128]{2,1,0:T(8,128)(2,1)} %p_hbm.1, f32[8,2,2048]{2,1,0:T(2,128)} %seed_hbm.1), custom_call_target="tpu_custom_call" | custom-call | tf_op jit(solution)/shard_map/pallas_call | solution.py:495
  39.5 1.5 %shard_map.87 = (f32[16,256,128]{2,1,0:T(8,128)}, f32[8,2,2048]{2,1,0:T(2,128)}) custom-call(f32[8,32,128]{2,1,0:T(8,128)S(1)} %get-tuple-element.7.q_ref, f32[16,256,128]{2,1,0:T(8,128)S(1)} %get-tuple-element.8.g_ref, f32[8,2,2048]{2,1,0:T(2,128)S(1)} %get-tuple-element.9.r_ref), custom_call_target="tpu_custom_call" | custom-call | tf_op jit(solution)/shard_map/pallas_call | solution.py:562
